TPU v7x, 32 devices: a whole 2x2x4 slice. The times are simulated.
32 devices in a mesh: img: 16 (over z, y, x), blk: 2 (over core).
Axes of the slice: x: 2, y: 2, z: 4, core: 2. Of those that a mesh axis runs over, the one named last changes fastest.
Arguments:
- descriptors: bfloat16 [64, 128, 256], P(('img', 'blk')), may hold values from -8 to 8
- covisible: int32 [64, 6], P(('img', 'blk')), may hold values from 0 to 63, as said below
- tile_counts: int32 [64], P(('img', 'blk')), may hold values from 1 to 6, as said below
- keypoints: int32 [64], replicated, may hold values from 32 to 128, as said below
- query_weight: bfloat16 [256, 256], replicated, may hold values from -0.375 to 0.375
- key_weight: bfloat16 [256, 256], replicated, may hold values from -0.375 to 0.375
- value_weight: bfloat16 [256, 256], replicated, may hold values from -0.375 to 0.375
- merge_weight: bfloat16 [512, 512], replicated, may hold values from -0.25 to 0.25
- output_weight: bfloat16 [512, 256], replicated, may hold values from -0.25 to 0.25
- dustbin: float32 [1], replicated, may hold values from 0.5 to 2
Outputs:
- plan: float32 [64, 6, 128, 128], P(('img', 'blk'))
- row_bin: float32 [64, 128], P(('img', 'blk'))
- col_bin: float32 [64, 128], P(('img', 'blk'))
Inputs may be any that keep to these rules, and one draw needn't show every extreme that they name: `covisible`: the 6 entries of a block's row name different blocks, never the block itself, all within its own image group of 4 consecutive blocks or the groups just before and after it. `tile_counts`: some block uses all 6 of its listed blocks. The valid keypoints of a block are its first ones; some block is full.
All inputs are finite; a program needn't handle non-finite values.
Results may differ from a plain program's by a relative error of at most 0.0032.
Values may be sent and summed in bfloat16 or wider, within the bound.
A program may use at most 64 MiB of HBM per device.

v0:
```python
import math

import jax
import jax.numpy as jnp
from jax import lax
from jax.sharding import PartitionSpec as P

HEADS = 4
ITERS = 3


def with_halo(block, sides, width):
    for axis, dim in sides:
        count = lax.axis_size(axis)
        forward = [(i, i + 1) for i in range(count - 1)]
        backward = [(target, source) for source, target in forward]
        low = lax.ppermute(
            lax.slice_in_dim(block, block.shape[dim] - width, None, axis=dim), axis, forward
        )
        high = lax.ppermute(lax.slice_in_dim(block, 0, width, axis=dim), axis, backward)
        block = jnp.concatenate([low, block, high], axis=dim)
    return block


def shifted_2(block, axis, distance):
    devices = range(lax.axis_size(axis))
    route = [(i - distance, i) for i in devices if i - distance in devices]
    return lax.ppermute(block, axis, route)


def project_rows(values, weight):
    flat = jnp.dot(values.reshape(-1, values.shape[-1]), weight, preferred_element_type=jnp.float32)
    return flat.reshape(values.shape[:-1] + (weight.shape[1],)).astype(jnp.bfloat16)


def on_device(
    descriptors,
    covisible,
    tile_counts,
    keypoints,
    query_weight,
    key_weight,
    value_weight,
    merge_weight,
    output_weight,
    dustbin,
):
    local_blocks, block_len, feature_dim = descriptors.shape
    head_dim = feature_dim // HEADS
    tile_count = covisible.shape[1]
    blk_count = lax.axis_size("blk")
    group_size = local_blocks * blk_count
    near_count = 3 * group_size
    group_index = lax.axis_index("img")
    blk_index = lax.axis_index("blk")
    first_block = (group_index - 1) * group_size
    near_ids = covisible - first_block
    padding = jnp.zeros((group_size,), jnp.int32)
    padded_counts = jnp.concatenate([padding, keypoints, padding])
    near_kpts = lax.dynamic_slice_in_dim(padded_counts, group_index * group_size, near_count)
    own_kpts = lax.dynamic_slice_in_dim(
        keypoints, (group_index * blk_count + blk_index) * local_blocks, local_blocks
    )
    slot_hit = near_ids[:, :, None] == jnp.arange(near_count, dtype=jnp.int32)[None, None, :]
    tile_kpts = jnp.sum(jnp.where(slot_hit, near_kpts[None, None, :], 0), axis=2)
    positions = jnp.arange(block_len, dtype=jnp.int32)
    tile_live = jnp.arange(tile_count, dtype=jnp.int32)[None, :] < tile_counts[:, None]
    key_live = tile_live[:, :, None] & (positions[None, None, :] < tile_kpts[:, :, None])
    row_live = positions[None, :] < own_kpts[:, None]
    query = project_rows(descriptors, query_weight)
    group_desc = lax.all_gather(descriptors, "blk", axis=0, tiled=True)
    near_desc = with_halo(group_desc, (("img", 0),), group_size)
    near_keys = project_rows(near_desc, key_weight)
    near_values = project_rows(near_desc, value_weight)
    key_tiles = jnp.take(near_keys, near_ids, axis=0).reshape(
        local_blocks, tile_count * block_len, HEADS, head_dim
    )
    value_tiles = jnp.take(near_values, near_ids, axis=0).reshape(
        local_blocks, tile_count * block_len, HEADS, head_dim
    )
    logits = jnp.einsum(
        "rqhd,rkhd->rhqk",
        query.reshape(local_blocks, block_len, HEADS, head_dim),
        key_tiles,
        preferred_element_type=jnp.float32,
    ) / math.sqrt(head_dim)
    logits = jnp.where(key_live.reshape(local_blocks, 1, 1, tile_count * block_len), logits, -1e30)
    highest = jnp.max(logits, axis=3, keepdims=True)
    weights = jnp.exp(logits - highest)
    weights = (weights / jnp.sum(weights, axis=3, keepdims=True)).astype(jnp.bfloat16)
    message = jnp.einsum(
        "rhqk,rkhd->rqhd", weights, value_tiles, preferred_element_type=jnp.float32
    )
    message = message.reshape(local_blocks, block_len, feature_dim).astype(jnp.bfloat16)
    joined = jnp.concatenate([descriptors, message], axis=2).reshape(-1, 2 * feature_dim)
    hidden = jnp.maximum(
        jnp.dot(joined, merge_weight, preferred_element_type=jnp.float32), 0.0
    ).astype(jnp.bfloat16)
    refined = descriptors.reshape(-1, feature_dim).astype(jnp.float32) + jnp.dot(
        hidden, output_weight, preferred_element_type=jnp.float32
    )
    refined = refined.astype(jnp.bfloat16).reshape(local_blocks, block_len, feature_dim)
    group_refined = lax.all_gather(refined, "blk", axis=0, tiled=True)
    near_refined = with_halo(group_refined, (("img", 0),), group_size)
    match_tiles = jnp.take(near_refined, near_ids, axis=0)
    scores = jnp.einsum(
        "rid,rkjd->rkij", refined, match_tiles, preferred_element_type=jnp.float32
    ) / math.sqrt(feature_dim)
    valid = tile_live[:, :, None, None] & row_live[:, None, :, None] & key_live[:, :, None, :]
    dust = dustbin[0]
    own_pot = jnp.zeros((local_blocks, block_len), jnp.float32)
    near_pot = jnp.zeros((near_count, block_len), jnp.float32)
    row_pot = jnp.zeros((local_blocks, block_len), jnp.float32)
    placing = slot_hit.reshape(local_blocks * tile_count, near_count).astype(jnp.float32)
    for sweep in range(ITERS):
        tile_pot = jnp.take(near_pot, near_ids, axis=0)
        shifted = jnp.where(valid, scores + tile_pot[:, :, None, :], -1e30)
        highest_row = jnp.maximum(jnp.max(shifted, axis=(1, 3)), dust)
        total = jnp.sum(jnp.exp(shifted - highest_row[:, None, :, None]), axis=(1, 3)) + jnp.exp(
            dust - highest_row
        )
        row_pot = -(highest_row + jnp.log(total))
        mass = jnp.sum(
            jnp.where(
                valid, jnp.exp(scores + row_pot[:, None, :, None] + tile_pot[:, :, None, :]), 0.0
            ),
            axis=2,
        )
        spread = jnp.dot(placing.T, mass.reshape(-1, block_len), precision=lax.Precision.HIGHEST)
        sections = spread.reshape(3, group_size, block_len)
        from_after = shifted_2(sections[0], "img", -1)
        from_before = shifted_2(sections[2], "img", 1)
        col_sum = lax.psum_scatter(
            sections[1] + from_after + from_before, "blk", scatter_dimension=0, tiled=True
        )
        own_pot = own_pot - jnp.log(col_sum + jnp.exp(dust + own_pot))
        group_pot = lax.all_gather(own_pot, "blk", axis=0, tiled=True)
        near_pot = with_halo(group_pot, (("img", 0),), group_size)
    tile_pot = jnp.take(near_pot, near_ids, axis=0)
    plan = jnp.where(valid, scores + row_pot[:, None, :, None] + tile_pot[:, :, None, :], 0.0)
    row_bin = jnp.where(row_live, dust + row_pot, 0.0)
    col_bin = jnp.where(row_live, dust + own_pot, 0.0)
    return (plan, row_bin, col_bin)


def solution(mesh):
    in_specs = (
        P(("img", "blk"), None, None),
        P(("img", "blk"), None),
        P(("img", "blk")),
        P(),
        P(),
        P(),
        P(),
        P(),
        P(),
        P(),
    )
    out_specs = (
        P(("img", "blk"), None, None, None),
        P(("img", "blk"), None),
        P(("img", "blk"), None),
    )
    return jax.shard_map(
        on_device, mesh=mesh, in_specs=in_specs, out_specs=out_specs, check_vma=False
    )
```

profile of v0, /device:TPU:8, one launch (start us, length us, event | category | flops | bytes accessed | tf_op | source)
XLA Modules:
  0.0 145.7 jit_solution(14355334630967252538)
XLA Ops:
  0.6 2.3 %all_gather.15 = bf16[4,128,256]{2,1,0:T(8,128)(2,1)S(1)} all-gather(bf16[2,128,256]{2,1,0:T(8,128)(2,1)} %param.14), channel_id=1, replica_groups=mesh['img'=16,'blk'=2] {'blk'}, dimensions={0}, use_global_device_ids=true | all-gather | bytes 393216 | tf_op jit(solution)/shard_map/all_gather | solution.py:71
  3.0 3.4 %collective-permute-start = (bf16[4,128,256]{2,1,0:T(8,128)(2,1)S(1)}, bf16[4,128,256]{2,1,0:T(8,128)(2,1)S(1)}, u32[]{:S(2)}, u32[]{:S(2)}) collective-permute-start(bf16[4,128,256]{2,1,0:T(8,128)(2,1)S(1)} %all_gather.15), channel_id=1, source_target_pairs={{0,2},{2,4},{4,6},{6,8},{8,10},{10,12},{12,14},{14,16},{16,18},{18... | collective-permute-start | bytes 786440 | tf_op jit(solution)/shard_map/ppermute | solution.py:17
  6.4 4.2 %collective-permute-start.1 = (bf16[4,128,256]{2,1,0:T(8,128)(2,1)S(1)}, bf16[4,128,256]{2,1,0:T(8,128)(2,1)S(1)}, u32[]{:S(2)}, u32[]{:S(2)}) collective-permute-start(bf16[4,128,256]{2,1,0:T(8,128)(2,1)S(1)} %all_gather.15), channel_id=1, source_target_pairs={{2,0},{4,2},{6,4},{8,6},{10,8},{12,10},{14,12},{16,14},{18,16},{20... | collective-permute-start | bytes 786440 | tf_op jit(solution)/shard_map/ppermute | solution.py:20
  25.9 2.0 %reshape.213 = bf16[2,768,4,64]{1,3,2,0:T(8,128)(2,1)S(1)} reshape(bf16[2,6,128,256]{2,1,3,0:T(8,128)(2,1)} %get-tuple-element.30) | data formatting | bytes 1572864 | tf_op jit(solution)/shard_map/reshape | solution.py:78
  27.9 2.0 %reshape.215 = bf16[2,768,4,64]{1,3,2,0:T(8,128)(2,1)S(1)} reshape(bf16[2,6,128,256]{2,1,3,0:T(8,128)(2,1)} %get-tuple-element.29) | data formatting | bytes 1572864 | tf_op jit(solution)/shard_map/reshape | solution.py:75
  30.0 2.8 %fusion.48 = (f32[2,4,128]{2,1,0:T(4,128)S(1)}, f32[2,4,128,768]{3,2,1,0:T(8,128)}) fusion(pred[2,768]{1,0:T(4,128)(4,1)S(1)} %copy-done.5, bf16[2,128,4,64]{1,3,2,0:T(8,128)(2,1)S(1)} %bitcast.111, bf16[2,768,4,64]{1,3,2,0:T(8,128)(2,1)S(1)} %reshape.215), kind=kOutput, calls=%fused_computation.118 | convolution fusion | flops 103809792 | bytes 4068864 | tf_op jit(solution)/shard_map/sub | solution.py:89
  32.8 2.7 %fusion.10 = bf16[2,4,64,128]{3,2,1,0:T(8,128)(2,1)S(1)} fusion(bf16[2,768,4,64]{1,3,2,0:T(8,128)(2,1)S(1)} %reshape.213, f32[2,4,128,768]{3,2,1,0:T(8,128)} %get-tuple-element.32, f32[2,4,128]{2,1,0:T(4,128)S(1)} %get-tuple-element.31), kind=kOutput, calls=%fused_computation.32 | convolution fusion | flops 102301696 | bytes 4067328 | tf_op jit(solution)/shard_map/rhqk,rkhd->rqhd/dot_general | solution.py:91
  38.2 2.7 %collective-permute-start.3 = (bf16[4,128,256]{2,1,0:T(8,128)(2,1)S(1)}, bf16[4,128,256]{2,1,0:T(8,128)(2,1)S(1)}, u32[]{:S(2)}, u32[]{:S(2)}) collective-permute-start(bf16[4,128,256]{2,1,0:T(8,128)(2,1)S(1)} %all_gather.16), channel_id=1, source_target_pairs={{2,0},{4,2},{6,4},{8,6},{10,8},{12,10},{14,12},{16,14},{18,16},{20... | collective-permute-start | bytes 786440 | tf_op jit(solution)/shard_map/ppermute | solution.py:20
  40.9 3.1 %collective-permute-start.2 = (bf16[4,128,256]{2,1,0:T(8,128)(2,1)S(1)}, bf16[4,128,256]{2,1,0:T(8,128)(2,1)S(1)}, u32[]{:S(2)}, u32[]{:S(2)}) collective-permute-start(bf16[4,128,256]{2,1,0:T(8,128)(2,1)S(1)} %all_gather.16), channel_id=1, source_target_pairs={{0,2},{2,4},{4,6},{6,8},{8,10},{10,12},{12,14},{14,16},{16,18},{18... | collective-permute-start | bytes 786440 | tf_op jit(solution)/shard_map/ppermute | solution.py:17
  45.3 3.9 %collective-permute-done.3 = bf16[4,128,256]{2,1,0:T(8,128)(2,1)S(1)} collective-permute-done((bf16[4,128,256]{2,1,0:T(8,128)(2,1)S(1)}, bf16[4,128,256]{2,1,0:T(8,128)(2,1)S(1)}, u32[]{:S(2)}, u32[]{:S(2)}) %collective-permute-start.3) | collective-permute-done | bytes 262176 | tf_op jit(solution)/shard_map/ppermute | solution.py:20
  49.3 4.1 %collective-permute-done.2 = bf16[4,128,256]{2,1,0:T(8,128)(2,1)S(1)} collective-permute-done((bf16[4,128,256]{2,1,0:T(8,128)(2,1)S(1)}, bf16[4,128,256]{2,1,0:T(8,128)(2,1)S(1)}, u32[]{:S(2)}, u32[]{:S(2)}) %collective-permute-start.2) | collective-permute-done | bytes 262176 | tf_op jit(solution)/shard_map/ppermute | solution.py:17
  56.8 4.4 %collective-permute-start.5 = (f32[4,128]{1,0:T(4,128)S(1)}, f32[4,128]{1,0:T(4,128)S(1)}, u32[]{:S(2)}, u32[]{:S(2)}) collective-permute-start(f32[4,128]{1,0:T(4,128)S(1)} %get-tuple-element.23), channel_id=1, source_target_pairs={{0,2},{2,4},{4,6},{6,8},{8,10},{10,12},{12,14},{14,16},{16,18},{18... | collective-permute-start | bytes 6152 | tf_op jit(solution)/shard_map/ppermute | solution.py:28
  61.2 3.3 %collective-permute-start.4 = (f32[4,128]{1,0:T(4,128)S(1)}, f32[4,128]{1,0:T(4,128)S(1)}, u32[]{:S(2)}, u32[]{:S(2)}) collective-permute-start(f32[4,128]{1,0:T(4,128)S(1)} %get-tuple-element.22), channel_id=1, source_target_pairs={{2,0},{4,2},{6,4},{8,6},{10,8},{12,10},{14,12},{16,14},{18,16},{20... | collective-permute-start | bytes 6152 | tf_op jit(solution)/shard_map/ppermute | solution.py:28
  66.7 2.4 %all-reduce = f32[4,128]{1,0:T(4,128)S(1)} all-reduce(f32[4,128]{1,0:T(4,128)S(1)} %fusion.32), channel_id=2, replica_groups=mesh['img'=16,'blk'=2] {'blk'}, use_global_device_ids=true, to_apply=%region_6.9.clone | all-reduce | flops 512 | bytes 4096
  70.9 5.0 %collective-permute-start.7 = (f32[4,128]{1,0:T(4,128)S(1)}, f32[4,128]{1,0:T(4,128)S(1)}, u32[]{:S(2)}, u32[]{:S(2)}) collective-permute-start(f32[4,128]{1,0:T(4,128)S(1)} %bitcast.114), channel_id=1, source_target_pairs={{2,0},{4,2},{6,4},{8,6},{10,8},{12,10},{14,12},{16,14},{18,16},{20... | collective-permute-start | bytes 6152 | tf_op jit(solution)/shard_map/ppermute | solution.py:20
  77.9 5.3 %collective-permute-done.6 = f32[4,128]{1,0:T(4,128)S(1)} collective-permute-done((f32[4,128]{1,0:T(4,128)S(1)}, f32[4,128]{1,0:T(4,128)S(1)}, u32[]{:S(2)}, u32[]{:S(2)}) %collective-permute-start.6) | collective-permute-done | bytes 2080 | tf_op jit(solution)/shard_map/ppermute | solution.py:17
  88.1 5.7 %collective-permute-start.8 = (f32[4,128]{1,0:T(4,128)S(1)}, f32[4,128]{1,0:T(4,128)S(1)}, u32[]{:S(2)}, u32[]{:S(2)}) collective-permute-start(f32[4,128]{1,0:T(4,128)S(1)} %get-tuple-element.20), channel_id=1, source_target_pairs={{2,0},{4,2},{6,4},{8,6},{10,8},{12,10},{14,12},{16,14},{18,16},{20... | collective-permute-start | bytes 6152 | tf_op jit(solution)/shard_map/ppermute | solution.py:28
  95.2 2.4 %all-reduce.1 = f32[4,128]{1,0:T(4,128)S(1)} all-reduce(f32[4,128]{1,0:T(4,128)S(1)} %fusion.31), channel_id=3, replica_groups=mesh['img'=16,'blk'=2] {'blk'}, use_global_device_ids=true, to_apply=%region_10.13.clone | all-reduce | flops 512 | bytes 4096
  99.4 6.0 %collective-permute-start.11 = (f32[4,128]{1,0:T(4,128)S(1)}, f32[4,128]{1,0:T(4,128)S(1)}, u32[]{:S(2)}, u32[]{:S(2)}) collective-permute-start(f32[4,128]{1,0:T(4,128)S(1)} %bitcast.120), channel_id=1, source_target_pairs={{2,0},{4,2},{6,4},{8,6},{10,8},{12,10},{14,12},{16,14},{18,16},{20... | collective-permute-start | bytes 6152 | tf_op jit(solution)/shard_map/ppermute | solution.py:20
  107.4 5.3 %collective-permute-done.10 = f32[4,128]{1,0:T(4,128)S(1)} collective-permute-done((f32[4,128]{1,0:T(4,128)S(1)}, f32[4,128]{1,0:T(4,128)S(1)}, u32[]{:S(2)}, u32[]{:S(2)}) %collective-permute-start.10) | collective-permute-done | bytes 2080 | tf_op jit(solution)/shard_map/ppermute | solution.py:17
  118.2 5.7 %collective-permute-start.12 = (f32[4,128]{1,0:T(4,128)S(1)}, f32[4,128]{1,0:T(4,128)S(1)}, u32[]{:S(2)}, u32[]{:S(2)}) collective-permute-start(f32[4,128]{1,0:T(4,128)S(1)} %get-tuple-element.18), channel_id=1, source_target_pairs={{2,0},{4,2},{6,4},{8,6},{10,8},{12,10},{14,12},{16,14},{18,16},{20... | collective-permute-start | bytes 6152 | tf_op jit(solution)/shard_map/ppermute | solution.py:28
  125.2 2.4 %all-reduce.2 = f32[4,128]{1,0:T(4,128)S(1)} all-reduce(f32[4,128]{1,0:T(4,128)S(1)} %fusion.30), channel_id=4, replica_groups=mesh['img'=16,'blk'=2] {'blk'}, use_global_device_ids=true, to_apply=%region_14.17.clone | all-reduce | flops 512 | bytes 4096
  130.1 6.0 %collective-permute-start.15 = (f32[4,128]{1,0:T(4,128)S(1)}, f32[4,128]{1,0:T(4,128)S(1)}, u32[]{:S(2)}, u32[]{:S(2)}) collective-permute-start(f32[4,128]{1,0:T(4,128)S(1)} %bitcast.117), channel_id=1, source_target_pairs={{2,0},{4,2},{6,4},{8,6},{10,8},{12,10},{14,12},{16,14},{18,16},{20... | collective-permute-start | bytes 6152 | tf_op jit(solution)/shard_map/ppermute | solution.py:20
  138.0 5.3 %collective-permute-done.14 = f32[4,128]{1,0:T(4,128)S(1)} collective-permute-done((f32[4,128]{1,0:T(4,128)S(1)}, f32[4,128]{1,0:T(4,128)S(1)}, u32[]{:S(2)}, u32[]{:S(2)}) %collective-permute-start.14) | collective-permute-done | bytes 2080 | tf_op jit(solution)/shard_map/ppermute | solution.py:17
  (118 shorter events, 50.3 us)
Async XLA Ops:
  0.6 35.1 %copy-start = (bf16[512,512]{1,0:T(8,128)(2,1)S(1)}, bf16[512,512]{1,0:T(8,128)(2,1)}, u32[]{:S(2)}) copy-start(bf16[512,512]{1,0:T(8,128)(2,1)} %param.21) | copy-start | bytes 1572868
  3.0 14.9 %collective-permute-start = (bf16[4,128,256]{2,1,0:T(8,128)(2,1)S(1)}, bf16[4,128,256]{2,1,0:T(8,128)(2,1)S(1)}, u32[]{:S(2)}, u32[]{:S(2)}) collective-permute-start(bf16[4,128,256]{2,1,0:T(8,128)(2,1)S(1)} %all_gather.15), channel_id=1, source_target_pairs={{0,2},{2,4},{4,6},{6,8},{8,10},{10,12},{12,14},{14,16},{16,18},{18... | collective-permute-start | bytes 786440 | tf_op jit(solution)/shard_map/ppermute | solution.py:17
  6.4 13.4 %collective-permute-start.1 = (bf16[4,128,256]{2,1,0:T(8,128)(2,1)S(1)}, bf16[4,128,256]{2,1,0:T(8,128)(2,1)S(1)}, u32[]{:S(2)}, u32[]{:S(2)}) collective-permute-start(bf16[4,128,256]{2,1,0:T(8,128)(2,1)S(1)} %all_gather.15), channel_id=1, source_target_pairs={{2,0},{4,2},{6,4},{8,6},{10,8},{12,10},{14,12},{16,14},{18,16},{20... | collective-permute-start | bytes 786440 | tf_op jit(solution)/shard_map/ppermute | solution.py:20
  11.3 4.6 %copy-start.3 = (s32[2,6]{1,0:T(2,128)}, s32[2,6]{1,0:T(2,128)S(1)}, u32[]{:S(2)}) copy-start(s32[2,6]{1,0:T(2,128)S(1)} %get-tuple-element.17) | copy-start | bytes 148
  17.9 4.6 %copy-start.2 = (bf16[256,256]{1,0:T(8,128)(2,1)S(1)}, bf16[256,256]{1,0:T(8,128)(2,1)}, u32[]{:S(2)}) copy-start(bf16[256,256]{1,0:T(8,128)(2,1)} %param.20) | copy-start | bytes 393220
  24.2 5.8 %copy-start.5 = (pred[2,768]{1,0:T(4,128)(4,1)S(1)}, pred[2,768]{1,0:T(4,128)(4,1)}, u32[]{:S(2)}) copy-start(pred[2,768]{1,0:T(4,128)(4,1)} %bitcast_and_fusion) | copy-start | bytes 4612
  32.8 2.9 %copy-start.8 = (bf16[512,256]{1,0:T(8,128)(2,1)S(1)}, bf16[512,256]{1,0:T(8,128)(2,1)}, u32[]{:S(2)}) copy-start(bf16[512,256]{1,0:T(8,128)(2,1)} %param.22) | copy-start | bytes 786436
  38.2 11.1 %collective-permute-start.3 = (bf16[4,128,256]{2,1,0:T(8,128)(2,1)S(1)}, bf16[4,128,256]{2,1,0:T(8,128)(2,1)S(1)}, u32[]{:S(2)}, u32[]{:S(2)}) collective-permute-start(bf16[4,128,256]{2,1,0:T(8,128)(2,1)S(1)} %all_gather.16), channel_id=1, source_target_pairs={{2,0},{4,2},{6,4},{8,6},{10,8},{12,10},{14,12},{16,14},{18,16},{20... | collective-permute-start | bytes 786440 | tf_op jit(solution)/shard_map/ppermute | solution.py:20
  40.9 12.5 %collective-permute-start.2 = (bf16[4,128,256]{2,1,0:T(8,128)(2,1)S(1)}, bf16[4,128,256]{2,1,0:T(8,128)(2,1)S(1)}, u32[]{:S(2)}, u32[]{:S(2)}) collective-permute-start(bf16[4,128,256]{2,1,0:T(8,128)(2,1)S(1)} %all_gather.16), channel_id=1, source_target_pairs={{0,2},{2,4},{4,6},{6,8},{8,10},{10,12},{12,14},{14,16},{16,18},{18... | collective-permute-start | bytes 786440 | tf_op jit(solution)/shard_map/ppermute | solution.py:17
  53.5 3.0 %copy-start.4 = (s32[2,6]{1,0:T(2,128)S(1)}, s32[2,6]{1,0:T(2,128)}, u32[]{:S(2)}) copy-start(s32[2,6]{1,0:T(2,128)} %copy-done.3) | copy-start | bytes 148
  53.5 11.0 %copy-start.9 = (u32[32]{0:T(128)S(1)}, u32[32]{0:T(128)}, u32[]{:S(2)}) copy-start(u32[32]{0:T(128)} %constant.62) | copy-start | bytes 388
  55.0 59.5 %copy-start.7 = (s32[2]{0:T(128)S(1)}, s32[2]{0:T(128)}, u32[]{:S(2)}) copy-start(s32[2]{0:T(128)} %copy-done.6) | copy-start | bytes 28
  56.8 8.9 %collective-permute-start.5 = (f32[4,128]{1,0:T(4,128)S(1)}, f32[4,128]{1,0:T(4,128)S(1)}, u32[]{:S(2)}, u32[]{:S(2)}) collective-permute-start(f32[4,128]{1,0:T(4,128)S(1)} %get-tuple-element.23), channel_id=1, source_target_pairs={{0,2},{2,4},{4,6},{6,8},{8,10},{10,12},{12,14},{14,16},{16,18},{18... | collective-permute-start | bytes 6152 | tf_op jit(solution)/shard_map/ppermute | solution.py:28
  61.2 5.5 %collective-permute-start.4 = (f32[4,128]{1,0:T(4,128)S(1)}, f32[4,128]{1,0:T(4,128)S(1)}, u32[]{:S(2)}, u32[]{:S(2)}) collective-permute-start(f32[4,128]{1,0:T(4,128)S(1)} %get-tuple-element.22), channel_id=1, source_target_pairs={{2,0},{4,2},{6,4},{8,6},{10,8},{12,10},{14,12},{16,14},{18,16},{20... | collective-permute-start | bytes 6152 | tf_op jit(solution)/shard_map/ppermute | solution.py:28
  70.9 7.0 %collective-permute-start.7 = (f32[4,128]{1,0:T(4,128)S(1)}, f32[4,128]{1,0:T(4,128)S(1)}, u32[]{:S(2)}, u32[]{:S(2)}) collective-permute-start(f32[4,128]{1,0:T(4,128)S(1)} %bitcast.114), channel_id=1, source_target_pairs={{2,0},{4,2},{6,4},{8,6},{10,8},{12,10},{14,12},{16,14},{18,16},{20... | collective-permute-start | bytes 6152 | tf_op jit(solution)/shard_map/ppermute | solution.py:20
  76.0 7.3 %collective-permute-start.6 = (f32[4,128]{1,0:T(4,128)S(1)}, f32[4,128]{1,0:T(4,128)S(1)}, u32[]{:S(2)}, u32[]{:S(2)}) collective-permute-start(f32[4,128]{1,0:T(4,128)S(1)} %bitcast.115), channel_id=1, source_target_pairs={{0,2},{2,4},{4,6},{6,8},{8,10},{10,12},{12,14},{14,16},{16,18},{18... | collective-permute-start | bytes 6152 | tf_op jit(solution)/shard_map/ppermute | solution.py:17
  86.2 7.7 %collective-permute-start.9 = (f32[4,128]{1,0:T(4,128)S(1)}, f32[4,128]{1,0:T(4,128)S(1)}, u32[]{:S(2)}, u32[]{:S(2)}) collective-permute-start(f32[4,128]{1,0:T(4,128)S(1)} %get-tuple-element.21), channel_id=1, source_target_pairs={{0,2},{2,4},{4,6},{6,8},{8,10},{10,12},{12,14},{14,16},{16,18},{18... | collective-permute-start | bytes 6152 | tf_op jit(solution)/shard_map/ppermute | solution.py:28
  88.1 7.0 %collective-permute-start.8 = (f32[4,128]{1,0:T(4,128)S(1)}, f32[4,128]{1,0:T(4,128)S(1)}, u32[]{:S(2)}, u32[]{:S(2)}) collective-permute-start(f32[4,128]{1,0:T(4,128)S(1)} %get-tuple-element.20), channel_id=1, source_target_pairs={{2,0},{4,2},{6,4},{8,6},{10,8},{12,10},{14,12},{16,14},{18,16},{20... | collective-permute-start | bytes 6152 | tf_op jit(solution)/shard_map/ppermute | solution.py:28
  99.4 7.9 %collective-permute-start.11 = (f32[4,128]{1,0:T(4,128)S(1)}, f32[4,128]{1,0:T(4,128)S(1)}, u32[]{:S(2)}, u32[]{:S(2)}) collective-permute-start(f32[4,128]{1,0:T(4,128)S(1)} %bitcast.120), channel_id=1, source_target_pairs={{2,0},{4,2},{6,4},{8,6},{10,8},{12,10},{14,12},{16,14},{18,16},{20... | collective-permute-start | bytes 6152 | tf_op jit(solution)/shard_map/ppermute | solution.py:20
  105.4 7.3 %collective-permute-start.10 = (f32[4,128]{1,0:T(4,128)S(1)}, f32[4,128]{1,0:T(4,128)S(1)}, u32[]{:S(2)}, u32[]{:S(2)}) collective-permute-start(f32[4,128]{1,0:T(4,128)S(1)} %bitcast.121), channel_id=1, source_target_pairs={{0,2},{2,4},{4,6},{6,8},{8,10},{10,12},{12,14},{14,16},{16,18},{18... | collective-permute-start | bytes 6152 | tf_op jit(solution)/shard_map/ppermute | solution.py:17
  116.3 7.7 %collective-permute-start.13 = (f32[4,128]{1,0:T(4,128)S(1)}, f32[4,128]{1,0:T(4,128)S(1)}, u32[]{:S(2)}, u32[]{:S(2)}) collective-permute-start(f32[4,128]{1,0:T(4,128)S(1)} %get-tuple-element.19), channel_id=1, source_target_pairs={{0,2},{2,4},{4,6},{6,8},{8,10},{10,12},{12,14},{14,16},{16,18},{18... | collective-permute-start | bytes 6152 | tf_op jit(solution)/shard_map/ppermute | solution.py:28
  118.2 7.0 %collective-permute-start.12 = (f32[4,128]{1,0:T(4,128)S(1)}, f32[4,128]{1,0:T(4,128)S(1)}, u32[]{:S(2)}, u32[]{:S(2)}) collective-permute-start(f32[4,128]{1,0:T(4,128)S(1)} %get-tuple-element.18), channel_id=1, source_target_pairs={{2,0},{4,2},{6,4},{8,6},{10,8},{12,10},{14,12},{16,14},{18,16},{20... | collective-permute-start | bytes 6152 | tf_op jit(solution)/shard_map/ppermute | solution.py:28
  130.1 7.9 %collective-permute-start.15 = (f32[4,128]{1,0:T(4,128)S(1)}, f32[4,128]{1,0:T(4,128)S(1)}, u32[]{:S(2)}, u32[]{:S(2)}) collective-permute-start(f32[4,128]{1,0:T(4,128)S(1)} %bitcast.117), channel_id=1, source_target_pairs={{2,0},{4,2},{6,4},{8,6},{10,8},{12,10},{14,12},{16,14},{18,16},{20... | collective-permute-start | bytes 6152 | tf_op jit(solution)/shard_map/ppermute | solution.py:20
  136.1 7.3 %collective-permute-start.14 = (f32[4,128]{1,0:T(4,128)S(1)}, f32[4,128]{1,0:T(4,128)S(1)}, u32[]{:S(2)}, u32[]{:S(2)}) collective-permute-start(f32[4,128]{1,0:T(4,128)S(1)} %bitcast.118), channel_id=1, source_target_pairs={{0,2},{2,4},{4,6},{6,8},{8,10},{10,12},{12,14},{14,16},{16,18},{18... | collective-permute-start | bytes 6152 | tf_op jit(solution)/shard_map/ppermute | solution.py:17
  (2 other events, 4.4 us)
where the time goes:
time: 146 us
  starting transfers between devices  59.1 us (40%)
  waiting for transfers between devices  31.2 us (21%)
  blocking collectives  17.1 us (12%)
  local copies, waits for them, and re-layouts  12.7 us (9%)
  other arithmetic  12.5 us (9%)
  matrix products  10.5 us (7%)
  between operations  2.57 us (2%)
    ppermute x5, starting transfers between devices, with_halo(): lax.ppermute(lax.slice_in_dim(block, 0, width, axis=dim), axis, backward)  23.9 us
    ppermute x6, starting transfers between devices, shifted_2(): return lax.ppermute(block, axis, route)  22.9 us
    ppermute x5, waiting for transfers between devices, with_halo(): lax.ppermute(lax.slice_in_dim(block, block.shape[dim] - width, None, axis...  22 us
    ppermute x5, starting transfers between devices, with_halo(): lax.ppermute(lax.slice_in_dim(block, block.shape[dim] - width, None, axis...  12.3 us
    unnamed x3, blocking collectives  7.33 us
    ppermute x5, waiting for transfers between devices, with_halo(): lax.ppermute(lax.slice_in_dim(block, 0, width, axis=dim), axis, backward)  5.77 us
    all_gather x3, blocking collectives, on_device(): group_pot = lax.all_gather(own_pot, 'blk', axis=0, tiled=True)  5.4 us
    ppermute x6, waiting for transfers between devices, shifted_2(): return lax.ppermute(block, axis, route)  3.48 us
  transfers between devices with their start and end apart: 16, of which 10 were waited for; matrix products, arithmetic and copies ran while one was open for 5% of the time, Pallas kernels for 0%

commit v1 on v0

v1 whole, which is shorter than its diff:
```python
import functools
import math

import jax
import jax.numpy as jnp
from jax import lax
from jax.experimental import pallas as pl
from jax.experimental.pallas import tpu as pltpu
from jax.sharding import PartitionSpec as P

HEADS = 4
ITERS = 3
DEAD = -1e30
MESH = pl.DeviceIdType.MESH


def kernel(
    img_count,
    blk_count,
    desc_ref,
    cov_ref,
    count_ref,
    kpt_ref,
    wq_ref,
    wk_ref,
    wv_ref,
    wm_ref,
    wo_ref,
    dust_ref,
    plan_ref,
    row_ref,
    col_ref,
    near_desc,
    near_ref,
    near_k,
    near_v,
    query,
    merged,
    scores,
    acc,
    mass_in,
    pot,
    desc_ssem,
    desc_rsem,
    ref_ssem,
    ref_rsem,
    mass_ssem,
    mass_rsem,
):
    local, block, width = desc_ref.shape
    tiles = cov_ref.shape[1]
    group = local * blk_count
    head_dim = width // HEADS
    img = lax.axis_index("img")
    blk = lax.axis_index("blk")
    others = [lax.rem(blk + step, blk_count) for step in range(1, blk_count)]
    first_block = (img - 1) * group

    def exists(shift):
        if shift == 0:
            return True
        return img + shift < img_count if shift > 0 else img + shift >= 0

    def guarded(shift, body):
        if shift == 0:
            body()
        else:
            pl.when(exists(shift))(body)

    barrier = pltpu.get_barrier_semaphore()
    for shift in range(-2, 3):
        def greet(shift=shift):
            for member in others if shift == 0 else range(blk_count):
                pl.semaphore_signal(
                    barrier, inc=1, device_id=(img + shift, member), device_id_type=MESH
                )
        guarded(shift, greet)

    def slot(near, section, member):
        return near.at[pl.ds((section * blk_count + member) * local, local)]

    def sender(source, near, ssem, rsem, section, shift, member):
        return pltpu.make_async_remote_copy(
            src_ref=source,
            dst_ref=slot(near, section, blk),
            send_sem=ssem.at[section, member],
            recv_sem=rsem.at[section, blk],
            device_id=(img + shift, member),
            device_id_type=MESH,
        )

    def arrival(near, ssem, rsem, section, member):
        here = slot(near, section, member)
        return pltpu.make_async_remote_copy(
            src_ref=here,
            dst_ref=here,
            send_sem=ssem.at[section, member],
            recv_sem=rsem.at[section, member],
            device_id=(img, others[0]),
            device_id_type=MESH,
        )

    def send_own(source, near, ssem, rsem):
        for shift in (1, -1):
            guarded(
                shift,
                lambda shift=shift: sender(
                    source, near, ssem, rsem, 1 - shift, shift, blk
                ).start(),
            )
        for member in others:
            sender(source, near, ssem, rsem, 1, 0, member).start()

    def relay(near, ssem, rsem, section):
        def body():
            arrival(near, ssem, rsem, section, blk).wait_recv()
            for member in others:
                sender(slot(near, section, blk), near, ssem, rsem, section, 0, member).start()
        guarded(section - 1, body)

    def wait_relayed(near, ssem, rsem, section, after=None):
        def body():
            for member in others:
                arrival(near, ssem, rsem, section, member).wait_recv()
                if after is not None:
                    after(section, member)
        guarded(section - 1, body)

    def drain(source, near, ssem, rsem):
        for shift in (1, -1):
            guarded(
                shift,
                lambda shift=shift: sender(
                    source, near, ssem, rsem, 1 - shift, shift, blk
                ).wait_send(),
            )
        for section in range(3):
            def body(section=section):
                for member in others:
                    sender(source, near, ssem, rsem, section, 0, member).wait_send()
            guarded(section - 1, body)

    def project(rows, section, member):
        where_to = pl.ds((section * blk_count + member) * local, local)
        for weight, target in ((wk_ref, near_k), (wv_ref, near_v)):
            out = jnp.dot(rows, weight[...], preferred_element_type=jnp.float32)
            target[where_to] = out.astype(jnp.bfloat16).reshape(local, block, width)

    def project_near(section, member):
        rows = near_desc[pl.ds((section * blk_count + member) * local, local)]
        project(rows.reshape(local * block, width), section, member)

    for source in range(-2, 3):
        if source != 0:
            @pl.when(jnp.logical_not(exists(source)))
            def _(source=source):
                for sweep in range(ITERS):
                    mass_in[sweep, source + 2] = jnp.zeros(mass_in.shape[2:], jnp.float32)

    own = desc_ref[...].reshape(local * block, width)
    low = jnp.maximum(img - 2, 0)
    high = jnp.minimum(img + 2, img_count - 1)
    pl.semaphore_wait(barrier, (high - low + 1) * blk_count - 1)
    send_own(desc_ref, near_desc, desc_ssem, desc_rsem)

    scaled = jnp.dot(own, wq_ref[...], preferred_element_type=jnp.float32) * (
        1.0 / math.sqrt(head_dim)
    )
    query[...] = scaled.astype(jnp.bfloat16).reshape(local, block, width)
    project(own, 1, blk)
    merged[...] = jnp.dot(
        own, wm_ref[pl.ds(0, width), :], preferred_element_type=jnp.float32
    ).reshape(merged.shape)
    wait_relayed(near_desc, desc_ssem, desc_rsem, 1, project_near)
    for section in (0, 2):
        relay(near_desc, desc_ssem, desc_rsem, section)
    for section in (0, 2):
        guarded(section - 1, lambda section=section: project_near(section, blk))
    for section in (0, 2):
        wait_relayed(near_desc, desc_ssem, desc_rsem, section, project_near)

    lanes = lax.broadcasted_iota(jnp.int32, (1, block), 1)
    rows_at = lax.broadcasted_iota(jnp.int32, (block, 1), 0)
    head_of = lax.broadcasted_iota(jnp.int32, (1, width), 1) // head_dim
    heads = [head_of == head for head in range(HEADS)]
    own_kpt = [kpt_ref[(img * blk_count + blk) * local + r] for r in range(local)]
    near_ids = [
        [jnp.clip(cov_ref[r, t] - first_block, 0, 3 * group - 1) for t in range(tiles)]
        for r in range(local)
    ]
    limits = [
        [
            jnp.where(t < count_ref[r], kpt_ref[jnp.clip(cov_ref[r, t], 0, kpt_ref.shape[0] - 1)], 0)
            for t in range(tiles)
        ]
        for r in range(local)
    ]
    biases = [
        [jnp.where(lanes < limits[r][t], 0.0, DEAD) for t in range(tiles)] for r in range(local)
    ]

    for r in range(local):
        keys = jnp.concatenate([near_k[near_ids[r][t]] for t in range(tiles)], axis=0)
        values = jnp.concatenate([near_v[near_ids[r][t]] for t in range(tiles)], axis=0)
        q = query[r]
        bias = jnp.concatenate(biases[r], axis=1)
        message = jnp.zeros((block, width), jnp.float32)
        for head in range(HEADS):
            logits = lax.dot_general(
                jnp.where(heads[head], q, jnp.zeros_like(q)),
                keys,
                (((1,), (1,)), ((), ())),
                preferred_element_type=jnp.float32,
            ) + bias
            weights = jnp.exp(logits - jnp.max(logits, axis=1, keepdims=True))
            weights = weights * (1.0 / jnp.sum(weights, axis=1, keepdims=True))
            out = jnp.dot(
                weights.astype(jnp.bfloat16), values, preferred_element_type=jnp.float32
            )
            message = jnp.where(heads[head], out, message)
        hidden = jnp.maximum(
            merged[r]
            + jnp.dot(
                message.astype(jnp.bfloat16),
                wm_ref[pl.ds(width, width), :],
                preferred_element_type=jnp.float32,
            ),
            0.0,
        ).astype(jnp.bfloat16)
        refined = desc_ref[r].astype(jnp.float32) + jnp.dot(
            hidden, wo_ref[...], preferred_element_type=jnp.float32
        )
        near_ref[group + blk * local + r] = refined.astype(jnp.bfloat16)

    own_slot = slot(near_ref, 1, blk)
    send_own(own_slot, near_ref, ref_ssem, ref_rsem)
    drain(desc_ref, near_desc, desc_ssem, desc_rsem)
    for section in (0, 2):
        relay(near_ref, ref_ssem, ref_rsem, section)
    for section in (1, 0, 2):
        wait_relayed(near_ref, ref_ssem, ref_rsem, section)

    dust = dust_ref[0]
    row_live = [rows_at < own_kpt[r] for r in range(local)]
    for r in range(local):
        mine = near_ref[group + blk * local + r] * jnp.asarray(
            1.0 / math.sqrt(width), jnp.bfloat16
        )
        row_bias = jnp.where(row_live[r], 0.0, DEAD)
        for t in range(tiles):
            out = lax.dot_general(
                mine,
                near_ref[near_ids[r][t]],
                (((1,), (1,)), ((), ())),
                preferred_element_type=jnp.float32,
            )
            scores[r, t] = out + (row_bias + biases[r][t])

    slots = lax.broadcasted_iota(jnp.int32, (group, 1), 0)
    pots = [jnp.zeros((group, block), jnp.float32)] * 3

    def mass_copy(sweep, shift, member):
        first, count = max(0, shift), 3 - abs(shift)
        return pltpu.make_async_remote_copy(
            src_ref=acc.at[sweep, pl.ds(first, count)],
            dst_ref=mass_in.at[sweep, 2 - shift, blk, pl.ds(first, count)],
            send_sem=mass_ssem.at[sweep, shift + 2, member],
            recv_sem=mass_rsem.at[sweep, 2 - shift, blk],
            device_id=(img + shift, member),
            device_id_type=MESH,
        )

    def mass_arrival(sweep, source, member):
        first, count = max(0, -source), 3 - abs(source)
        here = mass_in.at[sweep, source + 2, member, pl.ds(first, count)]
        return pltpu.make_async_remote_copy(
            src_ref=here,
            dst_ref=here,
            send_sem=mass_ssem.at[sweep, source + 2, member],
            recv_sem=mass_rsem.at[sweep, source + 2, member],
            device_id=(img, others[0]),
            device_id_type=MESH,
        )

    def each_partner(body):
        for shift in (-1, 1, -2, 2, 0):
            def run(shift=shift):
                for member in others if shift == 0 else range(blk_count):
                    body(shift, member)
            guarded(shift, run)

    row_pots = [None] * local
    for sweep in range(ITERS):
        spread = [jnp.zeros((group, block), jnp.float32)] * 3
        for r in range(local):
            def shifted(t):
                if sweep == 0:
                    return scores[r, t]
                return scores[r, t] + pot[pl.ds(near_ids[r][t], 1), :]
            top = shifted(0)
            for t in range(1, tiles):
                top = jnp.maximum(top, shifted(t))
            top = jnp.maximum(jnp.max(top, axis=1, keepdims=True), dust)
            terms = [jnp.exp(shifted(t) - top) for t in range(tiles)]
            total = functools.reduce(jnp.add, terms)
            total = jnp.sum(total, axis=1, keepdims=True) + jnp.exp(dust - top)
            row_pots[r] = -(top + jnp.log(total))
            inverse = 1.0 / total
            for t in range(tiles):
                mass = jnp.sum(terms[t] * inverse, axis=0, keepdims=True)
                for section in range(3):
                    hit = slots == near_ids[r][t] - section * group
                    spread[section] = spread[section] + jnp.where(hit, mass, 0.0)
        for section in range(3):
            acc[sweep, section] = spread[section]
        each_partner(lambda shift, member: mass_copy(sweep, shift, member).start())
        if sweep == 0:
            drain(own_slot, near_ref, ref_ssem, ref_rsem)
        if sweep == ITERS - 1:
            for r in range(local):
                row = jnp.broadcast_to(row_pots[r], (block, block))
                row = jnp.sum(jnp.where(rows_at == lanes, row, 0.0), axis=0, keepdims=True)
                row_ref[pl.ds(r, 1), :] = jnp.where(lanes < own_kpt[r], dust + row, 0.0)
                for t in range(tiles):
                    scores[r, t] = scores[r, t] + row_pots[r]
        sums = list(spread)
        each_partner(lambda source, member: mass_arrival(sweep, source, member).wait_recv())
        for source in range(-2, 3):
            for member in others if source == 0 else range(blk_count):
                for section in range(3):
                    if 0 <= section - source <= 2:
                        sums[section] = sums[section] + mass_in[
                            sweep, source + 2, member, section - source
                        ]
        for section in range(3):
            pots[section] = pots[section] - jnp.log(
                sums[section] + jnp.exp(dust + pots[section])
            )
            pot[pl.ds(section * group, group), :] = pots[section]

    for r in range(local):
        for t in range(tiles):
            out = scores[r, t] + pot[pl.ds(near_ids[r][t], 1), :]
            valid = jnp.where(row_live[r], lanes, block) < limits[r][t]
            plan_ref[r, t] = jnp.where(valid, out, 0.0)
        mine = pot[pl.ds(group + blk * local + r, 1), :]
        col_ref[pl.ds(r, 1), :] = jnp.where(lanes < own_kpt[r], dust + mine, 0.0)
    for sweep in range(ITERS):
        each_partner(lambda shift, member: mass_copy(sweep, shift, member).wait_send())


def on_device(
    img_count,
    blk_count,
    descriptors,
    covisible,
    tile_counts,
    keypoints,
    query_weight,
    key_weight,
    value_weight,
    merge_weight,
    output_weight,
    dustbin,
):
    local, block, width = descriptors.shape
    tiles = covisible.shape[1]
    group = local * blk_count
    near = 3 * group
    vmem = pl.BlockSpec(memory_space=pltpu.VMEM)
    smem = pl.BlockSpec(memory_space=pltpu.SMEM)
    dma = pltpu.SemaphoreType.DMA
    half = jnp.bfloat16
    full = jnp.float32
    return pl.pallas_call(
        functools.partial(kernel, img_count, blk_count),
        out_shape=(
            jax.ShapeDtypeStruct((local, tiles, block, block), full),
            jax.ShapeDtypeStruct((local, block), full),
            jax.ShapeDtypeStruct((local, block), full),
        ),
        in_specs=[vmem, smem, smem, smem, vmem, vmem, vmem, vmem, vmem, smem],
        out_specs=(vmem, vmem, vmem),
        scratch_shapes=[
            pltpu.VMEM((near, block, width), half),
            pltpu.VMEM((near, block, width), half),
            pltpu.VMEM((near, block, width), half),
            pltpu.VMEM((near, block, width), half),
            pltpu.VMEM((local, block, width), half),
            pltpu.VMEM((local, block, merge_weight.shape[1]), full),
            pltpu.VMEM((local, tiles, block, block), full),
            pltpu.VMEM((ITERS, 3, group, block), full),
            pltpu.VMEM((ITERS, 5, blk_count, 3, group, block), full),
            pltpu.VMEM((near, block), full),
            dma((3, blk_count)),
            dma((3, blk_count)),
            dma((3, blk_count)),
            dma((3, blk_count)),
            dma((ITERS, 5, blk_count)),
            dma((ITERS, 5, blk_count)),
        ],
        compiler_params=pltpu.CompilerParams(collective_id=0, has_side_effects=True),
    )(
        descriptors,
        covisible,
        tile_counts,
        keypoints,
        query_weight,
        key_weight,
        value_weight,
        merge_weight,
        output_weight,
        dustbin,
    )


def solution(mesh):
    in_specs = (
        P(("img", "blk"), None, None),
        P(("img", "blk"), None),
        P(("img", "blk")),
        P(),
        P(),
        P(),
        P(),
        P(),
        P(),
        P(),
    )
    out_specs = (
        P(("img", "blk"), None, None, None),
        P(("img", "blk"), None),
        P(("img", "blk"), None),
    )
    return jax.shard_map(
        functools.partial(on_device, mesh.shape["img"], mesh.shape["blk"]),
        mesh=mesh,
        in_specs=in_specs,
        out_specs=out_specs,
        check_vma=False,
    )
```

time: 146 us -> 44.5 us (0.30)
  the two profiles are of different devices: /device:TPU:8 before, /device:TPU:0 now
where the time goes in v1:
time: 44.5 us; the launch traced here: 44.3 us
  Pallas kernels  39.8 us (89%)
  local copies, waits for them, and re-layouts  3.27 us (7%)
  between operations  1.3 us (3%)
    pallas_call x1, Pallas kernels, on_device(): pl.pallas_call(functools.partial(kernel, img_count, blk_count), out_shape...  39.8 us
    unnamed x7, local copies, waits for them, and re-layouts  3.27 us

profile of v1, /device:TPU:0, one launch (start us, length us, event | category | flops | bytes accessed | tf_op | source)
XLA Modules:
  0.0 44.3 jit_solution(3504231550028578291)
XLA Ops:
  1.3 39.8 %shard_map.121 = (f32[2,6,128,128]{3,2,1,0:T(8,128)}, f32[2,128]{1,0:T(2,128)}, f32[2,128]{1,0:T(2,128)}) custom-call(bf16[2,128,256]{2,1,0:T(8,128)(2,1)} %desc_ref.1, s32[2,6]{1,0:T(2,128)} %cov_ref.1, s32[2]{0:T(128)} %count_ref.1, s32[64]{0:T(128)} %kpt_ref.1, bf16[256,256]{1,0:T(8,128)(2,1)} %wq_ref.1, bf16[256,256]{1,0:T(8,128)(2,1)} %wk_ref.1, ...), custom_call_target="tpu_custom_call" | custom-call | tf_op jit(solution)/shard_map/pallas_call | solution.py:375
  41.0 0.0 copy-start.1
  41.1 2.1 %copy.17 = f32[2,6,128,128]{3,2,1,0:T(8,128)} copy(f32[2,6,128,128]{3,2,1,0:T(8,128)} %get-tuple-element.6) | data formatting | bytes 1572864
  43.1 0.0 copy-done.1
  43.1 0.0 copy-start
  43.1 0.6 %copy.18 = f32[2,128]{1,0:T(2,128)} copy(f32[2,128]{1,0:T(2,128)S(1)} %copy-done.1) | data formatting | bytes 2048
  43.7 0.1 copy-done
  43.8 0.6 %copy.19 = f32[2,128]{1,0:T(2,128)} copy(f32[2,128]{1,0:T(2,128)S(1)} %copy-done) | data formatting | bytes 2048
Async XLA Ops:
  41.0 2.1 %copy-start.1 = (f32[2,128]{1,0:T(2,128)S(1)}, f32[2,128]{1,0:T(2,128)}, u32[]{:S(2)}) copy-start(f32[2,128]{1,0:T(2,128)} %get-tuple-element.7) | copy-start | bytes 3076
  43.1 0.6 %copy-start = (f32[2,128]{1,0:T(2,128)S(1)}, f32[2,128]{1,0:T(2,128)}, u32[]{:S(2)}) copy-start(f32[2,128]{1,0:T(2,128)} %get-tuple-element.8) | copy-start | bytes 3076

commit v2 on v1

--- a/solution.py
+++ b/solution.py
@@ -17,6 +17,19 @@
 def kernel(
     img_count,
     blk_count,
+    desc_in,
+    cov_in,
+    count_in,
+    kpt_in,
+    wq_in,
+    wk_in,
+    wv_in,
+    wm_in,
+    wo_in,
+    dust_in,
+    plan_ref,
+    row_ref,
+    col_ref,
     desc_ref,
     cov_ref,
     count_ref,
@@ -27,9 +40,7 @@
     wm_ref,
     wo_ref,
     dust_ref,
-    plan_ref,
-    row_ref,
-    col_ref,
+    load_sem,
     near_desc,
     near_ref,
     near_k,
@@ -67,6 +78,23 @@
         else:
             pl.when(exists(shift))(body)
 
+    pairs = (
+        (desc_in, desc_ref),
+        (wq_in, wq_ref),
+        (wk_in, wk_ref),
+        (wv_in, wv_ref),
+        (wm_in, wm_ref),
+        (cov_in, cov_ref),
+        (count_in, count_ref),
+        (kpt_in, kpt_ref),
+        (dust_in, dust_ref),
+        (wo_in, wo_ref),
+    )
+    loads = [
+        pltpu.make_async_copy(source, target, load_sem.at[place])
+        for place, (source, target) in enumerate(pairs)
+    ]
+
     barrier = pltpu.get_barrier_semaphore()
     for shift in range(-2, 3):
         def greet(shift=shift):
@@ -75,6 +103,9 @@
                     barrier, inc=1, device_id=(img + shift, member), device_id_type=MESH
                 )
         guarded(shift, greet)
+
+    for load in loads:
+        load.start()
 
     def slot(near, section, member):
         return near.at[pl.ds((section * blk_count + member) * local, local)]
@@ -157,11 +188,13 @@
                 for sweep in range(ITERS):
                     mass_in[sweep, source + 2] = jnp.zeros(mass_in.shape[2:], jnp.float32)
 
-    own = desc_ref[...].reshape(local * block, width)
     low = jnp.maximum(img - 2, 0)
     high = jnp.minimum(img + 2, img_count - 1)
     pl.semaphore_wait(barrier, (high - low + 1) * blk_count - 1)
-    send_own(desc_ref, near_desc, desc_ssem, desc_rsem)
+    send_own(desc_in, near_desc, desc_ssem, desc_rsem)
+    for load in loads:
+        load.wait()
+    own = desc_ref[...].reshape(local * block, width)
 
     scaled = jnp.dot(own, wq_ref[...], preferred_element_type=jnp.float32) * (
         1.0 / math.sqrt(head_dim)
@@ -234,7 +267,7 @@
 
     own_slot = slot(near_ref, 1, blk)
     send_own(own_slot, near_ref, ref_ssem, ref_rsem)
-    drain(desc_ref, near_desc, desc_ssem, desc_rsem)
+    drain(desc_in, near_desc, desc_ssem, desc_rsem)
     for section in (0, 2):
         relay(near_ref, ref_ssem, ref_rsem, section)
     for section in (1, 0, 2):
@@ -368,7 +401,7 @@
     group = local * blk_count
     near = 3 * group
     vmem = pl.BlockSpec(memory_space=pltpu.VMEM)
-    smem = pl.BlockSpec(memory_space=pltpu.SMEM)
+    hbm = pl.BlockSpec(memory_space=pltpu.HBM)
     dma = pltpu.SemaphoreType.DMA
     half = jnp.bfloat16
     full = jnp.float32
@@ -379,9 +412,20 @@
             jax.ShapeDtypeStruct((local, block), full),
             jax.ShapeDtypeStruct((local, block), full),
         ),
-        in_specs=[vmem, smem, smem, smem, vmem, vmem, vmem, vmem, vmem, smem],
+        in_specs=[hbm] * 10,
         out_specs=(vmem, vmem, vmem),
         scratch_shapes=[
+            pltpu.VMEM(descriptors.shape, half),
+            pltpu.SMEM(covisible.shape, jnp.int32),
+            pltpu.SMEM(tile_counts.shape, jnp.int32),
+            pltpu.SMEM(keypoints.shape, jnp.int32),
+            pltpu.VMEM(query_weight.shape, half),
+            pltpu.VMEM(key_weight.shape, half),
+            pltpu.VMEM(value_weight.shape, half),
+            pltpu.VMEM(merge_weight.shape, half),
+            pltpu.VMEM(output_weight.shape, half),
+            pltpu.SMEM(dustbin.shape, full),
+            dma((10,)),
             pltpu.VMEM((near, block, width), half),
             pltpu.VMEM((near, block, width), half),
             pltpu.VMEM((near, block, width), half),
@@ -399,7 +443,9 @@
             dma((ITERS, 5, blk_count)),
             dma((ITERS, 5, blk_count)),
         ],
-        compiler_params=pltpu.CompilerParams(collective_id=0, has_side_effects=True),
+        compiler_params=pltpu.CompilerParams(
+            collective_id=0, has_side_effects=True
+        ),
     )(
         descriptors,
         covisible,

time: 44.5 us -> 43.4 us (0.975)
  Pallas kernels: 39.8 us -> 38.7 us
    pallas_call x1, Pallas kernels: 39.8 us -> 38.7 us  [on_device(): pl.pallas_call(functools.partial(kernel, img_count, blk_count), out_shape...]
where the time goes in v2:
time: 43.4 us; the launch traced here: 43.2 us
  Pallas kernels  38.7 us (89%)
  local copies, waits for them, and re-layouts  3.27 us (8%)
  between operations  1.3 us (3%)
    pallas_call x1, Pallas kernels, on_device(): pl.pallas_call(functools.partial(kernel, img_count, blk_count), out_shape...  38.7 us
    unnamed x7, local copies, waits for them, and re-layouts  3.27 us

profile of v2, /device:TPU:0, one launch (start us, length us, event | category | flops | bytes accessed | tf_op | source)
XLA Modules:
  0.0 43.2 jit_solution(15279784106596354566)
XLA Ops:
  1.3 38.7 %shard_map.121 = (f32[2,6,128,128]{3,2,1,0:T(8,128)}, f32[2,128]{1,0:T(2,128)}, f32[2,128]{1,0:T(2,128)}) custom-call(bf16[2,128,256]{2,1,0:T(8,128)(2,1)} %desc_in.1, s32[2,6]{1,0:T(2,128)} %cov_in.1, s32[2]{0:T(128)} %count_in.1, s32[64]{0:T(128)} %kpt_in.1, bf16[256,256]{1,0:T(8,128)(2,1)} %wq_in.1, bf16[256,256]{1,0:T(8,128)(2,1)} %wk_in.1, ...), custom_call_target="tpu_custom_call" | custom-call | tf_op jit(solution)/shard_map/pallas_call | solution.py:408
  39.9 0.0 copy-start.1
  40.0 2.1 %copy.17 = f32[2,6,128,128]{3,2,1,0:T(8,128)} copy(f32[2,6,128,128]{3,2,1,0:T(8,128)} %get-tuple-element.6) | data formatting | bytes 1572864
  42.0 0.0 copy-done.1
  42.0 0.0 copy-start
  42.0 0.6 %copy.18 = f32[2,128]{1,0:T(2,128)} copy(f32[2,128]{1,0:T(2,128)S(1)} %copy-done.1) | data formatting | bytes 2048
  42.6 0.1 copy-done
  42.7 0.6 %copy.19 = f32[2,128]{1,0:T(2,128)} copy(f32[2,128]{1,0:T(2,128)S(1)} %copy-done) | data formatting | bytes 2048
Async XLA Ops:
  39.9 2.1 %copy-start.1 = (f32[2,128]{1,0:T(2,128)S(1)}, f32[2,128]{1,0:T(2,128)}, u32[]{:S(2)}) copy-start(f32[2,128]{1,0:T(2,128)} %get-tuple-element.7) | copy-start | bytes 3076
  42.0 0.6 %copy-start = (f32[2,128]{1,0:T(2,128)S(1)}, f32[2,128]{1,0:T(2,128)}, u32[]{:S(2)}) copy-start(f32[2,128]{1,0:T(2,128)} %get-tuple-element.8) | copy-start | bytes 3076

commit v3 on v2

--- a/solution.py
+++ b/solution.py
@@ -27,9 +27,8 @@
     wm_in,
     wo_in,
     dust_in,
-    plan_ref,
-    row_ref,
-    col_ref,
+    base_out,
+    tail_ref,
     desc_ref,
     cov_ref,
     count_ref,
@@ -41,6 +40,7 @@
     wo_ref,
     dust_ref,
     load_sem,
+    base_sem,
     near_desc,
     near_ref,
     near_k,
@@ -321,6 +321,9 @@
                 for member in others if shift == 0 else range(blk_count):
                     body(shift, member)
             guarded(shift, run)
+
+    def base_copy(r, t):
+        return pltpu.make_async_copy(scores.at[r, t], base_out.at[r, t], base_sem.at[r, t])
 
     row_pots = [None] * local
     for sweep in range(ITERS):
@@ -353,9 +356,10 @@
             for r in range(local):
                 row = jnp.broadcast_to(row_pots[r], (block, block))
                 row = jnp.sum(jnp.where(rows_at == lanes, row, 0.0), axis=0, keepdims=True)
-                row_ref[pl.ds(r, 1), :] = jnp.where(lanes < own_kpt[r], dust + row, 0.0)
+                tail_ref[pl.ds(local * tiles + r, 1), :] = jnp.where(lanes < own_kpt[r], dust + row, 0.0)
                 for t in range(tiles):
                     scores[r, t] = scores[r, t] + row_pots[r]
+                    base_copy(r, t).start()
         sums = list(spread)
         each_partner(lambda source, member: mass_arrival(sweep, source, member).wait_recv())
         for source in range(-2, 3):
@@ -373,13 +377,51 @@
 
     for r in range(local):
         for t in range(tiles):
-            out = scores[r, t] + pot[pl.ds(near_ids[r][t], 1), :]
-            valid = jnp.where(row_live[r], lanes, block) < limits[r][t]
-            plan_ref[r, t] = jnp.where(valid, out, 0.0)
+            tail_ref[pl.ds(r * tiles + t, 1), :] = pot[pl.ds(near_ids[r][t], 1), :]
         mine = pot[pl.ds(group + blk * local + r, 1), :]
-        col_ref[pl.ds(r, 1), :] = jnp.where(lanes < own_kpt[r], dust + mine, 0.0)
+        tail_ref[pl.ds(local * (tiles + 1) + r, 1), :] = jnp.where(lanes < own_kpt[r], dust + mine, 0.0)
     for sweep in range(ITERS):
         each_partner(lambda shift, member: mass_copy(sweep, shift, member).wait_send())
+    for r in range(local):
+        for t in range(tiles):
+            base_copy(r, t).wait()
+
+
+def finish(
+    base_in, tail_in, plan_out, row_out, col_out, tail_ref, taken, made, in_sem, out_sem, end_sem
+):
+    local, tiles = base_in.shape[:2]
+    places = [(r, t) for r in range(local) for t in range(tiles)]
+
+    def fetch(r, t):
+        return pltpu.make_async_copy(base_in.at[r, t], taken.at[r, t], in_sem.at[r, t])
+
+    def put(r, t):
+        return pltpu.make_async_copy(made.at[r, t], plan_out.at[r, t], out_sem.at[r, t])
+
+    head = pltpu.make_async_copy(tail_in, tail_ref, end_sem.at[0])
+    head.start()
+    for place in places:
+        fetch(*place).start()
+    head.wait()
+    ends = [
+        pltpu.make_async_copy(
+            tail_ref.at[pl.ds(local * (tiles + step), local)], target, end_sem.at[1 + step]
+        )
+        for step, target in enumerate((row_out, col_out))
+    ]
+    for end in ends:
+        end.start()
+    for r, t in places:
+        fetch(r, t).wait()
+        base = taken[r, t]
+        out = base + tail_ref[pl.ds(r * tiles + t, 1), :]
+        made[r, t] = jnp.where(base > 0.1 * DEAD, out, 0.0)
+        put(r, t).start()
+    for place in places:
+        put(*place).wait()
+    for end in ends:
+        end.wait()
 
 
 def on_device(
@@ -405,15 +447,14 @@
     dma = pltpu.SemaphoreType.DMA
     half = jnp.bfloat16
     full = jnp.float32
-    return pl.pallas_call(
+    base, tail = pl.pallas_call(
         functools.partial(kernel, img_count, blk_count),
         out_shape=(
             jax.ShapeDtypeStruct((local, tiles, block, block), full),
-            jax.ShapeDtypeStruct((local, block), full),
-            jax.ShapeDtypeStruct((local, block), full),
+            jax.ShapeDtypeStruct((local * (tiles + 2), block), full),
         ),
         in_specs=[hbm] * 10,
-        out_specs=(vmem, vmem, vmem),
+        out_specs=(hbm, vmem),
         scratch_shapes=[
             pltpu.VMEM(descriptors.shape, half),
             pltpu.SMEM(covisible.shape, jnp.int32),
@@ -426,6 +467,7 @@
             pltpu.VMEM(output_weight.shape, half),
             pltpu.SMEM(dustbin.shape, full),
             dma((10,)),
+            dma((descriptors.shape[0], tiles)),
             pltpu.VMEM((near, block, width), half),
             pltpu.VMEM((near, block, width), half),
             pltpu.VMEM((near, block, width), half),
@@ -458,6 +500,24 @@
         output_weight,
         dustbin,
     )
+    return pl.pallas_call(
+        finish,
+        out_shape=(
+            jax.ShapeDtypeStruct(base.shape, full),
+            jax.ShapeDtypeStruct((local, block), full),
+            jax.ShapeDtypeStruct((local, block), full),
+        ),
+        in_specs=[hbm, hbm],
+        out_specs=(hbm, hbm, hbm),
+        scratch_shapes=[
+            pltpu.VMEM(tail.shape, full),
+            pltpu.VMEM(base.shape, full),
+            pltpu.VMEM(base.shape, full),
+            dma((local, tiles)),
+            dma((local, tiles)),
+            dma((3,)),
+        ],
+    )(base, tail)
 
 
 def solution(mesh):

time: 43.4 us -> 42 us (0.968)
  local copies, waits for them, and re-layouts: 3.27 us -> 0 us
  Pallas kernels: 38.7 us -> 40.5 us
    unnamed x7 -> x0, local copies, waits for them, and re-layouts: 3.27 us -> none
    pallas_call x0 -> x1, Pallas kernels: none -> 2.12 us  [on_device(): pl.pallas_call(finish, out_shape=(jax.ShapeDtypeStruct(base.shape, full),...]
where the time goes in v3:
time: 42 us; the launch traced here: 41.8 us
  Pallas kernels  40.5 us (96%)
  between operations  1.29 us (3%)
    pallas_call x1, Pallas kernels, on_device(): pl.pallas_call(functools.partial(kernel, img_count, blk_count), out_shape...  38.4 us
    pallas_call x1, Pallas kernels, on_device(): pl.pallas_call(finish, out_shape=(jax.ShapeDtypeStruct(base.shape, full),...  2.12 us

profile of v3, /device:TPU:0, one launch (start us, length us, event | category | flops | bytes accessed | tf_op | source)
XLA Modules:
  0.0 41.8 jit_solution(17022557867428104466)
XLA Ops:
  1.3 38.4 %shard_map.121 = (f32[2,6,128,128]{3,2,1,0:T(8,128)}, f32[16,128]{1,0:T(8,128)}) custom-call(bf16[2,128,256]{2,1,0:T(8,128)(2,1)} %desc_in.1, s32[2,6]{1,0:T(2,128)} %cov_in.1, s32[2]{0:T(128)} %count_in.1, s32[64]{0:T(128)} %kpt_in.1, bf16[256,256]{1,0:T(8,128)(2,1)} %wq_in.1, bf16[256,256]{1,0:T(8,128)(2,1)} %wk_in.1, bf16[256,256]{1,0:T(8,128)(2,1)} %wv_in.1, ...), custom_call_target="tpu_custom_call" | custom-call | tf_op jit(solution)/shard_map/pallas_call | solution.py:450
  39.7 2.1 %shard_map.122 = (f32[2,6,128,128]{3,2,1,0:T(8,128)}, f32[2,128]{1,0:T(2,128)}, f32[2,128]{1,0:T(2,128)}) custom-call(f32[2,6,128,128]{3,2,1,0:T(8,128)} %get-tuple-element.5.base_in, f32[16,128]{1,0:T(8,128)} %get-tuple-element.6.tail_in), custom_call_target="tpu_custom_call" | custom-call | tf_op jit(solution)/shard_map/pallas_call | solution.py:503

commit v4 on v3

--- a/solution.py
+++ b/solution.py
@@ -237,20 +237,22 @@
         values = jnp.concatenate([near_v[near_ids[r][t]] for t in range(tiles)], axis=0)
         q = query[r]
         bias = jnp.concatenate(biases[r], axis=1)
+        spans = [jnp.where(hit, q, jnp.zeros_like(q)) for hit in heads]
+        stacked = lax.dot_general(
+            jnp.concatenate(spans, axis=0),
+            keys,
+            (((1,), (1,)), ((), ())),
+            preferred_element_type=jnp.float32,
+        )
         message = jnp.zeros((block, width), jnp.float32)
         for head in range(HEADS):
-            logits = lax.dot_general(
-                jnp.where(heads[head], q, jnp.zeros_like(q)),
-                keys,
-                (((1,), (1,)), ((), ())),
-                preferred_element_type=jnp.float32,
-            ) + bias
+            logits = stacked[head * block : (head + 1) * block] + bias
             weights = jnp.exp(logits - jnp.max(logits, axis=1, keepdims=True))
-            weights = weights * (1.0 / jnp.sum(weights, axis=1, keepdims=True))
+            inverse = 1.0 / jnp.sum(weights, axis=1, keepdims=True)
             out = jnp.dot(
                 weights.astype(jnp.bfloat16), values, preferred_element_type=jnp.float32
             )
-            message = jnp.where(heads[head], out, message)
+            message = jnp.where(heads[head], out * inverse, message)
         hidden = jnp.maximum(
             merged[r]
             + jnp.dot(

time: 42 us -> 39.7 us (0.945)
  Pallas kernels: 40.5 us -> 38.3 us
    pallas_call x1, Pallas kernels: 38.4 us -> 36.1 us  [on_device(): pl.pallas_call(functools.partial(kernel, img_count, blk_count), out_shape...]
where the time goes in v4:
time: 39.7 us; the launch traced here: 39.6 us
  Pallas kernels  38.3 us (96%)
  between operations  1.29 us (3%)
    pallas_call x1, Pallas kernels, on_device(): pl.pallas_call(functools.partial(kernel, img_count, blk_count), out_shape...  36.1 us
    pallas_call x1, Pallas kernels, on_device(): pl.pallas_call(finish, out_shape=(jax.ShapeDtypeStruct(base.shape, full),...  2.12 us

profile of v4, /device:TPU:0, one launch (start us, length us, event | category | flops | bytes accessed | tf_op | source)
XLA Modules:
  0.0 39.6 jit_solution(8582232265168315056)
XLA Ops:
  1.3 36.1 %shard_map.121 = (f32[2,6,128,128]{3,2,1,0:T(8,128)}, f32[16,128]{1,0:T(8,128)}) custom-call(bf16[2,128,256]{2,1,0:T(8,128)(2,1)} %desc_in.1, s32[2,6]{1,0:T(2,128)} %cov_in.1, s32[2]{0:T(128)} %count_in.1, s32[64]{0:T(128)} %kpt_in.1, bf16[256,256]{1,0:T(8,128)(2,1)} %wq_in.1, bf16[256,256]{1,0:T(8,128)(2,1)} %wk_in.1, bf16[256,256]{1,0:T(8,128)(2,1)} %wv_in.1, ...), custom_call_target="tpu_custom_call" | custom-call | tf_op jit(solution)/shard_map/pallas_call | solution.py:452
  37.4 2.1 %shard_map.122 = (f32[2,6,128,128]{3,2,1,0:T(8,128)}, f32[2,128]{1,0:T(2,128)}, f32[2,128]{1,0:T(2,128)}) custom-call(f32[2,6,128,128]{3,2,1,0:T(8,128)} %get-tuple-element.5.base_in, f32[16,128]{1,0:T(8,128)} %get-tuple-element.6.tail_in), custom_call_target="tpu_custom_call" | custom-call | tf_op jit(solution)/shard_map/pallas_call | solution.py:505
